TPU v7x, 256 devices: a whole 4x4x8 slice. The times are simulated.
256 devices in a mesh: ctx: 16 (over z, x_hi), head: 16 (over x_lo, y, core).
Axes of the slice: x: 4 (x_hi: 2, x_lo: 2; x = x_hi * 2 + x_lo), y: 4, z: 8, core: 2. Of those that a mesh axis runs over, the one named last changes fastest.
Arguments:
- hidden: bfloat16 [16384, 8192], P('ctx', 'head'), may hold values from -6 to 6
- query_frozen_projection: bfloat16 [16384, 8192], P('ctx', 'head'), may hold values from -20 to 20
- key_projected: bfloat16 [16384, 1024], P('ctx'), may hold values from -20 to 20
- value_frozen_projection: bfloat16 [16384, 1024], P('ctx'), may hold values from -6 to 6
- query_down_factor: bfloat16 [8192, 16], P('head'), may hold values from -0.0625 to 0.0625
- query_up_factor: bfloat16 [16, 8192], P(None, 'head'), may hold values from -1.5 to 1.5
- value_down_factor: bfloat16 [8192, 16], P('head'), may hold values from -0.0625 to 0.0625
- value_up_factor: bfloat16 [16, 1024], replicated, may hold values from -1.5 to 1.5
- output_gradient: bfloat16 [16384, 8192], P('ctx', 'head'), may hold values from -0.046875 to 0.046875
- head_shift_mask: int32 [64], P('head'), may hold values from 0 to 1, as said below
Outputs:
- grad_a_q: float32 [8192, 16], P('head')
- query_up_gradient: float32 [16, 8192], P(None, 'head')
- grad_a_v: float32 [8192, 16], P('head')
- value_up_gradient: float32 [16, 1024], replicated
Inputs may be any that keep to these rules, and one draw needn't show every extreme that they name: `head_shift_mask`: exactly 32 of the heads carry 1.
All inputs are finite; a program needn't handle non-finite values.
Results may differ from a plain program's by a relative error of at most 0.0173.
The roundings to bfloat16 on the way count: a program that leaves them out, or rounds other values in their place, can miss the bound.
Values may be sent and summed in bfloat16 or wider, within the bound.
A program may use at most 128 MiB of HBM per device.

v0:
```python
import jax
import jax.numpy as jnp
from jax import lax
from jax.sharding import PartitionSpec as P

QUERY_HEADS = 64
KEY_VALUE_HEADS = 8
HEAD_SIZE = 128
adapter_scale = 2.0
pos_interp = 32.0
rope_base = 10000.0


def passed_along(block, axis, distance):
    devices = range(lax.axis_size(axis))
    route = [((i - distance) % len(devices), i) for i in devices]
    return lax.ppermute(block, axis, route)


def rope_tables(positions, head_width):
    half_width = head_width // 2
    inv_freq = rope_base ** (-(jnp.arange(half_width, dtype=jnp.float32) * 2.0 / head_width))
    angles = (positions.astype(jnp.float32) / pos_interp)[:, None] * inv_freq[None, :]
    return (jnp.cos(angles), jnp.sin(angles))


def rotate(tensor, cosine, sine_table):
    half_width = tensor.shape[-1] // 2
    first_half = tensor[..., :half_width]
    second_half = tensor[..., half_width:]
    return jnp.concatenate(
        [
            first_half * cosine - second_half * sine_table,
            second_half * cosine + first_half * sine_table,
        ],
        axis=-1,
    )


def unrotate(tensor, cosine, sine_table):
    half_width = tensor.shape[-1] // 2
    first_half = tensor[..., :half_width]
    second_half = tensor[..., half_width:]
    return jnp.concatenate(
        [
            first_half * cosine + second_half * sine_table,
            second_half * cosine - first_half * sine_table,
        ],
        axis=-1,
    )


def group_grads(query_rows, key_rows, value_rows, upstream):
    scale_factor = query_rows.shape[-1] ** (-0.5)
    scores = jnp.dot(query_rows, key_rows.T, preferred_element_type=jnp.float32) * scale_factor
    row_ids = lax.broadcasted_iota(jnp.int32, scores.shape, 0)
    col_ids = lax.broadcasted_iota(jnp.int32, scores.shape, 1)
    scores = jnp.where(col_ids <= row_ids, scores, -1e30)
    row_peak = jnp.max(scores, axis=1, keepdims=True)
    weights = jnp.exp(scores - row_peak)
    probs = weights / jnp.sum(weights, axis=1, keepdims=True)
    probs_low = probs.astype(jnp.bfloat16)
    output = jnp.dot(probs_low, value_rows, preferred_element_type=jnp.float32)
    delta = jnp.sum(upstream.astype(jnp.float32) * output, axis=1, keepdims=True)
    prob_grad = jnp.dot(upstream, value_rows.T, preferred_element_type=jnp.float32)
    score_grad = (probs * (prob_grad - delta)).astype(jnp.bfloat16)
    query_grad = jnp.dot(score_grad, key_rows, preferred_element_type=jnp.float32) * scale_factor
    value_gradient_total = jnp.dot(probs_low.T, upstream, preferred_element_type=jnp.float32)
    return (query_grad, value_gradient_total)


def regroup(own_rows, next_rows, head_mask):
    half_rows = next_rows.shape[0]
    shifted = jnp.concatenate([own_rows[half_rows:], next_rows], axis=0)
    return jnp.where(head_mask, shifted, own_rows)


def split_rows(gradient, head_mask, half_rows):
    lower_rows = gradient[:, :half_rows]
    upper_rows = gradient[:, half_rows:]
    own_part = jnp.where(
        head_mask, jnp.concatenate([jnp.zeros_like(lower_rows), lower_rows], axis=1), gradient
    )
    send_part = jnp.where(head_mask, upper_rows, jnp.zeros_like(upper_rows))
    return (own_part, send_part)


def on_device(
    hidden,
    query_frozen_projection,
    key_projected,
    value_frozen_projection,
    query_down_factor,
    query_up_factor,
    value_down_factor,
    value_up_factor,
    output_gradient,
    head_shift_mask,
):
    highest_precision = lax.Precision.HIGHEST
    group_rows = hidden.shape[0]
    half_rows = group_rows // 2
    heads_here = head_shift_mask.shape[0]
    adapter_rank_width = query_down_factor.shape[1]
    per_kv = QUERY_HEADS // KEY_VALUE_HEADS
    local_key_value_heads = max(1, heads_here // per_kv)
    fan_out = heads_here // local_key_value_heads
    ctx_number = lax.axis_index("ctx")
    head_number = lax.axis_index("head")
    first_key_value_head = head_number * heads_here // per_kv
    query_partial_sum = jnp.dot(hidden, query_down_factor, preferred_element_type=jnp.float32)
    value_partial_sum = jnp.dot(hidden, value_down_factor, preferred_element_type=jnp.float32)
    summed_q, summed_v = lax.psum((query_partial_sum, value_partial_sum), "head")
    query_upstream = summed_q.astype(jnp.bfloat16)
    value_upstream = summed_v.astype(jnp.bfloat16)
    own_pos = ctx_number * group_rows + jnp.arange(group_rows, dtype=jnp.int32)
    cosine, sine_table = rope_tables(own_pos, HEAD_SIZE)
    cos_rows = cosine[:, None, :]
    sin_rows = sine_table[:, None, :]
    query_before_rotary = query_frozen_projection.astype(jnp.float32) + adapter_scale * jnp.dot(
        query_upstream.astype(jnp.float32),
        query_up_factor.astype(jnp.float32),
        precision=highest_precision,
    )
    query_rows = rotate(
        query_before_rotary.reshape(group_rows, heads_here, HEAD_SIZE), cos_rows, sin_rows
    ).astype(jnp.bfloat16)
    key_cols = lax.dynamic_slice_in_dim(
        key_projected, first_key_value_head * HEAD_SIZE, local_key_value_heads * HEAD_SIZE, 1
    )
    key_rows = rotate(
        key_cols.astype(jnp.float32).reshape(group_rows, local_key_value_heads, HEAD_SIZE),
        cos_rows,
        sin_rows,
    ).astype(jnp.bfloat16)
    value_up_local = lax.dynamic_slice_in_dim(
        value_up_factor, first_key_value_head * HEAD_SIZE, local_key_value_heads * HEAD_SIZE, 1
    )
    value_columns = lax.dynamic_slice_in_dim(
        value_frozen_projection,
        first_key_value_head * HEAD_SIZE,
        local_key_value_heads * HEAD_SIZE,
        1,
    )
    value_before_adapter = value_columns.astype(jnp.float32) + adapter_scale * jnp.dot(
        value_upstream.astype(jnp.float32),
        value_up_local.astype(jnp.float32),
        precision=highest_precision,
    )
    value_rows = value_before_adapter.astype(jnp.bfloat16).reshape(
        group_rows, local_key_value_heads, HEAD_SIZE
    )
    upstream = output_gradient.reshape(group_rows, heads_here, HEAD_SIZE)
    head_flags = head_shift_mask > 0
    token_mask = head_flags[None, :, None]
    stack_mask = head_flags[:, None, None]
    next_query, next_keys, next_values, next_upstream = passed_along(
        (
            query_rows[:half_rows],
            key_rows[:half_rows],
            value_rows[:half_rows],
            upstream[:half_rows],
        ),
        "ctx",
        -1,
    )
    group_query = regroup(query_rows, next_query, token_mask)
    group_keys = regroup(
        jnp.repeat(key_rows, fan_out, axis=1), jnp.repeat(next_keys, fan_out, axis=1), token_mask
    )
    group_values = regroup(
        jnp.repeat(value_rows, fan_out, axis=1),
        jnp.repeat(next_values, fan_out, axis=1),
        token_mask,
    )
    group_upstream = regroup(upstream, next_upstream, token_mask)
    stacked = (
        jnp.moveaxis(group_query, 1, 0),
        jnp.moveaxis(group_keys, 1, 0),
        jnp.moveaxis(group_values, 1, 0),
        jnp.moveaxis(group_upstream, 1, 0),
    )
    query_grads, value_grads = lax.map(
        lambda members: group_grads(members[0], members[1], members[2], members[3]), stacked
    )
    own_query, send_query = split_rows(query_grads, stack_mask, half_rows)
    own_value, send_value = split_rows(value_grads, stack_mask, half_rows)
    own_value_kv = own_value.reshape(local_key_value_heads, fan_out, group_rows, HEAD_SIZE).sum(
        axis=1
    )
    send_value_kv = send_value.reshape(local_key_value_heads, fan_out, half_rows, HEAD_SIZE).sum(
        axis=1
    )
    back_query, back_value = passed_along((send_query, send_value_kv), "ctx", 1)
    own_query = own_query.at[:, :half_rows].add(back_query)
    own_value_kv = own_value_kv.at[:, :half_rows].add(back_value)
    prior_gradient = unrotate(jnp.moveaxis(own_query, 0, 1), cos_rows, sin_rows).reshape(
        group_rows, heads_here * HEAD_SIZE
    )
    value_token_rows = jnp.moveaxis(own_value_kv, 0, 1).reshape(
        group_rows, local_key_value_heads * HEAD_SIZE
    )
    query_up_gradient_piece = adapter_scale * jnp.dot(
        query_upstream.astype(jnp.float32).T, prior_gradient, precision=highest_precision
    )
    value_gradient_piece = adapter_scale * jnp.dot(
        value_upstream.astype(jnp.float32).T, value_token_rows, precision=highest_precision
    )
    token_query_piece = adapter_scale * jnp.dot(
        prior_gradient, query_up_factor.astype(jnp.float32).T, precision=highest_precision
    )
    token_value_piece = adapter_scale * jnp.dot(
        value_token_rows, value_up_local.astype(jnp.float32).T, precision=highest_precision
    )
    value_full = lax.dynamic_update_slice_in_dim(
        jnp.zeros((adapter_rank_width, KEY_VALUE_HEADS * HEAD_SIZE), jnp.float32),
        value_gradient_piece,
        first_key_value_head * HEAD_SIZE,
        1,
    )
    token_query_gradient, token_value_gradient = lax.psum(
        (token_query_piece, token_value_piece), "head"
    )
    a_q_part = jnp.dot(
        hidden.T, token_query_gradient.astype(jnp.bfloat16), preferred_element_type=jnp.float32
    )
    a_v_part = jnp.dot(
        hidden.T, token_value_gradient.astype(jnp.bfloat16), preferred_element_type=jnp.float32
    )
    grad_a_q, grad_a_v, query_up_gradient = lax.psum(
        (a_q_part, a_v_part, query_up_gradient_piece), "ctx"
    )
    value_up_gradient = lax.psum(value_full, ("ctx", "head"))
    return (grad_a_q, query_up_gradient, grad_a_v, value_up_gradient)


def solution(mesh):
    return jax.shard_map(
        on_device,
        mesh=mesh,
        in_specs=(
            P("ctx", "head"),
            P("ctx", "head"),
            P("ctx", None),
            P("ctx", None),
            P("head", None),
            P(None, "head"),
            P("head", None),
            P(),
            P("ctx", "head"),
            P("head"),
        ),
        out_specs=(P("head", None), P(None, "head"), P("head", None), P()),
        check_vma=False,
    )
```

profile of v0, /device:TPU:8, one launch (start us, length us, event | category | flops | bytes accessed | tf_op | source)
XLA Modules:
  0.0 588.5 jit_solution(2511384332108965878)
XLA Ops:
  8.4 2.4 fusion.51
  11.6 8.3 %collective-permute-start.1 = (bf16[512,1,128]{2,0,1:T(8,128)(2,1)}, bf16[512,1,128]{2,0,1:T(8,128)(2,1)}, u32[]{:S(2)}, u32[]{:S(2)}) collective-permute-start(bf16[512,1,128]{2,0,1:T(8,128)(2,1)} %pad_maximum_fusion.3), channel_id=1, source_target_pairs={{16,0},{32,16},{48,32},{64,48},{80,64},{96,80},{112,96},{128,112},... | collective-permute-start | bytes 393224 | tf_op jit(solution)/shard_map/ppermute | solution.py:17
  19.9 1.8 multiply_cosine_fusion.1
  23.0 52.5 %all-reduce.13 = (bf16[1024,16]{0,1:T(8,128)(2,1)S(1)}, bf16[1024,16]{0,1:T(8,128)(2,1)}) all-reduce(f32[1024,16]{0,1:T(8,128)S(1)} %fusion.72, f32[1024,16]{0,1:T(8,128)S(1)} %fusion.73), channel_id=1, replica_groups=mesh['ctx'=16,'head'=16] {'head'}, use_global_device_ids=true, to_apply=%region_0.1 | all-reduce | flops 32768 | bytes 196608 | tf_op jit(solution)/shard_map/psum | solution.py:113
  78.1 2.0 collective-permute-start
  82.6 2.0 collective-permute-start.2
  87.3 2.0 collective-permute-start.3
  89.3 1.8 copy.47
  95.5 1.8 copy.41
  101.9 2.0 collective-permute-done.3
  108.5 4.5 fusion.45
  113.1 45.1 %while.14 = (s32[]{:T(128)}, f32[4,1024,128]{1,2,0:T(8,128)}, f32[4,1024,128]{1,2,0:T(8,128)}, bf16[4,1024,128]{1,2,0:T(8,128)(2,1)}, bf16[4,1024,128]{1,2,0:T(8...) while((s32[]{:T(128)}, f32[4,1024,128]{1,2,0:T(8,128)}, ...), condition=%wide.region_6.7_spmd, body=%wide.region_2.6_spmd.sunk | while | flops 1373107200 | bytes 51430568 | solution.py:183
  113.1 1.8 fusion.111
  119.3 4.0 fusion.114
  130.6 4.0 fusion.114
  141.9 4.0 fusion.114
  153.2 4.0 fusion.114
  158.2 3.8 select_reduce_fusion.1
  162.0 2.0 collective-permute-start.4
  164.8 10.0 %collective-permute-done.5 = f32[1,512,128]{1,2,0:T(8,128)S(1)} collective-permute-done((f32[1,512,128]{1,2,0:T(8,128)S(1)}, f32[1,512,128]{1,2,0:T(8,128)S(1)}, u32[]{:S(2)}, u32[]{:S(2)}) %collective-permute-start.5) | collective-permute-done | bytes 262176 | tf_op jit(solution)/shard_map/ppermute | solution.py:17
  178.4 13.2 %collective-permute-done.4 = f32[4,512,128]{1,2,0:T(8,128)} collective-permute-done((f32[4,512,128]{1,2,0:T(8,128)}, f32[4,512,128]{1,2,0:T(8,128)}, u32[]{:S(2)}, u32[]{:S(2)}) %collective-permute-start.4) | collective-permute-done | bytes 1048608 | tf_op jit(solution)/shard_map/ppermute | solution.py:17
  196.2 61.3 %all-reduce.14 = (bf16[1024,16]{0,1:T(8,128)(2,1)S(1)}, bf16[1024,16]{0,1:T(8,128)(2,1)S(1)}) all-reduce(f32[1024,16]{0,1:T(8,128)S(1)} %convolution_multiply_fusion.2, f32[1024,16]{0,1:T(8,128)S(1)} %convolution_multiply_fusion.3), channel_id=1, replica_groups=mesh['ctx'=16,'head'=16] {'head'}, use_global_device_ids=true, to_apply=%region_7.8 | all-reduce | flops 32768 | bytes 196608 | tf_op jit(solution)/shard_map/psum | solution.py:221
  259.3 158.1 %all-reduce.10.cloned.1.call-done = f32[16,1024]{1,0:T(8,128)} async-done(((f32[16,1024]{1,0:T(8,128)}), f32[16,1024]{1,0:T(8,128)}) %all-reduce.10.cloned.1.call-update) | async-done | bytes 65552 | tf_op jit(solution)/shard_map/psum | solution.py:233
  417.4 158.7 %all-reduce.12.cloned.1.call-done = (f32[512,16]{0,1:T(8,128)}, f32[16,512]{1,0:T(8,128)}, f32[512,16]{0,1:T(8,128)}) async-done(((f32[512,16]{0,1:T(8,128)}, f32[16,512]{1,0:T(8,128)}, f32[512,16]{0,1:T(8,128)}), (f32[512,16]{0,1:T(8,128)}, f32[16,512]{1,0:T(8,128)}, f32[512,16]{0,1:T(8,128)})) %all-reduce.12.cloned.1.call-update) | async-done | bytes 98320 | tf_op jit(solution)/shard_map/psum | solution.py:230
  (148 shorter events, 68.0 us)
Async XLA Ops:
  7.2 14.5 %copy-start = (bf16[1024,512]{1,0:T(8,128)(2,1)S(1)}, bf16[1024,512]{1,0:T(8,128)(2,1)}, u32[]{:S(2)}) copy-start(bf16[1024,512]{1,0:T(8,128)(2,1)} %param.16) | copy-start | bytes 3145732
  7.2 14.5 %copy-start.24 = (bf16[512,16]{0,1:T(8,128)(2,1)S(1)}, bf16[512,16]{0,1:T(8,128)(2,1)}, u32[]{:S(2)}) copy-start(bf16[512,16]{0,1:T(8,128)(2,1)} %param.20) | copy-start | bytes 49156
  7.2 410.2 %all-reduce.10.cloned.1.call-start = ((), (), s32[]{:S(2)}) async-start(), calls=%async_computation | async-start | bytes 131072 | tf_op jit(solution)/shard_map/psum | solution.py:233
  8.4 13.7 %copy-start.25 = (bf16[512,16]{0,1:T(8,128)(2,1)S(1)}, bf16[512,16]{0,1:T(8,128)(2,1)}, u32[]{:S(2)}) copy-start(bf16[512,16]{0,1:T(8,128)(2,1)} %param.22) | copy-start | bytes 49156
  10.8 11.3 %copy-start.5 = (bf16[1024,1,64]{2,0,1:T(8,128)(2,1)}, bf16[1024,1,64]{2,0,1:T(8,128)(2,1)S(1)}, u32[]{:S(2)}) copy-start(bf16[1024,1,64]{2,0,1:T(8,128)(2,1)S(1)} %get-tuple-element.118) | copy-start | bytes 393220
  10.8 11.7 %copy-start.15 = (bf16[1024,512]{1,0:T(8,128)(2,1)S(1)}, bf16[1024,512]{1,0:T(8,128)(2,1)}, u32[]{:S(2)}) copy-start(bf16[1024,512]{1,0:T(8,128)(2,1)} %param.17) | copy-start | bytes 3145732
  11.6 88.6 %collective-permute-start.1 = (bf16[512,1,128]{2,0,1:T(8,128)(2,1)}, bf16[512,1,128]{2,0,1:T(8,128)(2,1)}, u32[]{:S(2)}, u32[]{:S(2)}) collective-permute-start(bf16[512,1,128]{2,0,1:T(8,128)(2,1)} %pad_maximum_fusion.3), channel_id=1, source_target_pairs={{16,0},{32,16},{48,32},{64,48},{80,64},{96,80},{112,96},{128,112},... | collective-permute-start | bytes 393224 | tf_op jit(solution)/shard_map/ppermute | solution.py:17
  21.7 53.8 %copy-start.23 = (bf16[16,512]{1,0:T(8,128)(2,1)S(1)}, bf16[16,512]{1,0:T(8,128)(2,1)}, u32[]{:S(2)}) copy-start(bf16[16,512]{1,0:T(8,128)(2,1)} %param.21) | copy-start | bytes 49156
  78.1 6.5 %copy-start.21 = (bf16[1024,16]{0,1:T(8,128)(2,1)S(1)}, bf16[1024,16]{0,1:T(8,128)(2,1)}, u32[]{:S(2)}) copy-start(bf16[1024,16]{0,1:T(8,128)(2,1)} %get-tuple-element.99) | copy-start | bytes 98308
  78.1 27.4 %collective-permute-start = (bf16[512,4,128]{0,2,1:T(8,128)(2,1)}, bf16[512,4,128]{0,2,1:T(8,128)(2,1)}, u32[]{:S(2)}, u32[]{:S(2)}) collective-permute-start(bf16[512,4,128]{0,2,1:T(8,128)(2,1)} %get-tuple-element.116), channel_id=1, source_target_pairs={{16,0},{32,16},{48,32},{64,48},{80,64},{96,80},{112,96},{128,112},... | collective-permute-start | bytes 1572872 | tf_op jit(solution)/shard_map/ppermute | solution.py:17
  82.6 22.9 %collective-permute-start.2 = (bf16[512,4,128]{0,2,1:T(8,128)(2,1)}, bf16[512,4,128]{0,2,1:T(8,128)(2,1)}, u32[]{:S(2)}, u32[]{:S(2)}) collective-permute-start(bf16[512,4,128]{0,2,1:T(8,128)(2,1)} %bitcast.15), channel_id=1, source_target_pairs={{16,0},{32,16},{48,32},{64,48},{80,64},{96,80},{112,96},{128,112},... | collective-permute-start | bytes 1572872 | tf_op jit(solution)/shard_map/ppermute | solution.py:17
  87.3 16.6 %collective-permute-start.3 = (bf16[512,1,128]{2,0,1:T(8,128)(2,1)}, bf16[512,1,128]{2,0,1:T(8,128)(2,1)}, u32[]{:S(2)}, u32[]{:S(2)}) collective-permute-start(bf16[512,1,128]{2,0,1:T(8,128)(2,1)} %get-tuple-element.120), channel_id=1, source_target_pairs={{16,0},{32,16},{48,32},{64,48},{80,64},{96,80},{112,96},{128,112},... | collective-permute-start | bytes 393224 | tf_op jit(solution)/shard_map/ppermute | solution.py:17
  95.5 13.0 %copy-start.13 = (bf16[1024,128]{0,1:T(8,128)(2,1)S(1)}, bf16[1024,128]{0,1:T(8,128)(2,1)}, u32[]{:S(2)}) copy-start(bf16[1024,128]{0,1:T(8,128)(2,1)} %copy.47) | copy-start | bytes 786436
  113.1 45.1 %copy-start.27 = (pred[4]{0:T(512)(128)(4,1)S(1)}, pred[4]{0:T(512)(128)(4,1)}, u32[]{:S(2)}) copy-start(pred[4]{0:T(512)(128)(4,1)} %broadcast_compare_fusion) | copy-start | bytes 16
  114.9 3.7 copy-start.1
  148.7 3.7 copy-start.1
  158.2 5.8 copy-start.2
  158.2 5.8 copy-start.3
  162.0 12.8 %collective-permute-start.5 = (f32[1,512,128]{1,2,0:T(8,128)S(1)}, f32[1,512,128]{1,2,0:T(8,128)S(1)}, u32[]{:S(2)}, u32[]{:S(2)}) collective-permute-start(f32[1,512,128]{1,2,0:T(8,128)S(1)} %bitcast.125), channel_id=1, source_target_pairs={{240,0},{0,16},{16,32},{32,48},{48,64},{64,80},{80,96},{96,112},{1... | collective-permute-start | bytes 786440 | tf_op jit(solution)/shard_map/ppermute | solution.py:17
  162.0 29.6 %collective-permute-start.4 = (f32[4,512,128]{1,2,0:T(8,128)}, f32[4,512,128]{1,2,0:T(8,128)}, u32[]{:S(2)}, u32[]{:S(2)}) collective-permute-start(f32[4,512,128]{1,2,0:T(8,128)} %get-tuple-element.124), channel_id=1, source_target_pairs={{240,0},{0,16},{16,32},{32,48},{48,64},{64,80},{80,96},{96,112},{1... | collective-permute-start | bytes 3145736 | tf_op jit(solution)/shard_map/ppermute | solution.py:17
  164.0 11.6 %copy-start.22 = (bf16[1024,16]{0,1:T(8,128)(2,1)S(1)}, bf16[1024,16]{0,1:T(8,128)(2,1)}, u32[]{:S(2)}) copy-start(bf16[1024,16]{0,1:T(8,128)(2,1)} %get-tuple-element.99) | copy-start | bytes 98308
  175.7 17.5 %copy-start.7 = (f32[1024,64]{0,1:T(8,128)S(1)}, f32[1024,64]{0,1:T(8,128)}, u32[]{:S(2)}) copy-start(f32[1024,64]{0,1:T(8,128)} %get-tuple-element.121) | copy-start | bytes 786436
  176.7 399.4 %all-reduce.12.cloned.1.call-start = ((), (), s32[]{:S(2)}) async-start(), calls=%async_computation.1 | async-start | bytes 196608 | tf_op jit(solution)/shard_map/psum | solution.py:230
  177.0 16.2 %copy-start.9 = (f32[1024,64]{0,1:T(8,128)S(1)}, f32[1024,64]{0,1:T(8,128)}, u32[]{:S(2)}) copy-start(f32[1024,64]{0,1:T(8,128)} %get-tuple-element.122) | copy-start | bytes 786436
  (21 other events, 39.9 us)
Sparse Core Ops, SparseCore 0:
  176.8 240.5 all-reduce.9
  420.8 155.2 all-reduce.11
where the time goes:
time: 590 us; the launch traced here: 589 us
  waiting for transfers between devices  342 us (58%)
  blocking collectives  114 us (19%)
  matrix products  41.3 us (7%)
  local copies, waits for them, and re-layouts  34.7 us (6%)
  other arithmetic  25.5 us (4%)
  starting transfers between devices  16.6 us (3%)
  between operations  14.4 us (2%)
    psum x1, waiting for transfers between devices, on_device(): lax.psum((a_q_part, a_v_part, query_up_gradient_piece), 'ctx')  159 us
    psum x1, waiting for transfers between devices, on_device(): value_up_gradient = lax.psum(value_full, ('ctx', 'head'))  158 us
    psum x1, blocking collectives, on_device(): lax.psum((token_query_piece, token_value_piece), 'head')  61.3 us
    psum x1, blocking collectives, on_device(): lax.psum((query_partial_sum, value_partial_sum), 'head')  52.5 us
    ppermute x6, waiting for transfers between devices, passed_along(): return lax.ppermute(block, axis, route)  25.2 us
    ppermute x6, starting transfers between devices, passed_along(): return lax.ppermute(block, axis, route)  16.3 us
    dot_general x4, matrix products, group_grads(): jnp.dot(score_grad, key_rows, preferred_element_type=jnp.float32)  15.8 us
  transfers between devices with their start and end apart: 8, of which 5 were waited for; matrix products, arithmetic and copies ran while one was open for 6% of the time, Pallas kernels for 0%

commit v1 on v0

--- a/solution.py
+++ b/solution.py
@@ -230,7 +230,7 @@
     grad_a_q, grad_a_v, query_up_gradient = lax.psum(
         (a_q_part, a_v_part, query_up_gradient_piece), "ctx"
     )
-    value_up_gradient = lax.psum(value_full, ("ctx", "head"))
+    value_up_gradient = jnp.sum(lax.all_gather(value_full, axis_name=("ctx", "head")), 0)
     return (grad_a_q, query_up_gradient, grad_a_v, value_up_gradient)
 
 

time: 590 us -> 448 us (0.76)
  waiting for transfers between devices: 342 us -> 181 us
  matrix products: 41.3 us -> 55.3 us
    psum x1 -> x0, waiting for transfers between devices: 158 us -> none  [on_device(): value_up_gradient = lax.psum(value_full, ('ctx', 'head'))]
    psum x1, waiting for transfers between devices: 159 us -> 117 us  [on_device(): lax.psum((a_q_part, a_v_part, query_up_gradient_piece), 'ctx')]
    all_gather x0 -> x1, waiting for transfers between devices: none -> 35.9 us  [on_device(): lax.all_gather(value_full, axis_name=('ctx', 'head'))]
    dot_general x4, matrix products: 6.81 us -> 15.7 us  [group_grads(): jnp.dot(probs_low.T, upstream, preferred_element_type=jnp.float32)]
    reduce_sum x0 -> x1, other arithmetic: none -> 7.31 us  [on_device(): jnp.sum(lax.all_gather(value_full, axis_name=('ctx', 'head')), 0)]
  transfers between devices with their start and end apart: 8 -> 8, of which waited for: 5 -> 4; matrix products, arithmetic and copies ran while one was open for 6% -> 9% of each run, Pallas kernels for 0% -> 0%
where the time goes in v1:
time: 448 us; the launch traced here: 447 us
  waiting for transfers between devices  181 us (40%)
  blocking collectives  114 us (25%)
  matrix products  55.3 us (12%)
  local copies, waits for them, and re-layouts  33.9 us (8%)
  other arithmetic  30.6 us (7%)
  starting transfers between devices  16.3 us (4%)
  between operations  15.9 us (4%)
    psum x1, waiting for transfers between devices, on_device(): lax.psum((a_q_part, a_v_part, query_up_gradient_piece), 'ctx')  117 us
    psum x1, blocking collectives, on_device(): lax.psum((token_query_piece, token_value_piece), 'head')  60.8 us
    psum x1, blocking collectives, on_device(): lax.psum((query_partial_sum, value_partial_sum), 'head')  53.1 us
    all_gather x1, waiting for transfers between devices, on_device(): lax.all_gather(value_full, axis_name=('ctx', 'head'))  35.9 us
    ppermute x6, waiting for transfers between devices, passed_along(): return lax.ppermute(block, axis, route)  27.5 us
    ppermute x6, starting transfers between devices, passed_along(): return lax.ppermute(block, axis, route)  16.2 us
    dot_general x4, matrix products, group_grads(): jnp.dot(score_grad, key_rows, preferred_element_type=jnp.float32)  15.8 us
    dot_general x4, matrix products, group_grads(): jnp.dot(probs_low.T, upstream, preferred_element_type=jnp.float32)  15.7 us
  transfers between devices with their start and end apart: 8, of which 4 were waited for; matrix products, arithmetic and copies ran while one was open for 9% of the time, Pallas kernels for 0%

profile of v1, /device:TPU:8, one launch (start us, length us, event | category | flops | bytes accessed | tf_op | source)
XLA Modules:
  0.0 446.9 jit_solution(8621361392438261842)
XLA Ops:
  11.4 53.1 %all-reduce.10 = (bf16[1024,16]{0,1:T(8,128)(2,1)S(1)}, bf16[1024,16]{0,1:T(8,128)(2,1)S(1)}) all-reduce(f32[1024,16]{0,1:T(8,128)S(1)} %fusion.73, f32[1024,16]{0,1:T(8,128)S(1)} %fusion.74), channel_id=1, replica_groups=mesh['ctx'=16,'head'=16] {'head'}, use_global_device_ids=true, to_apply=%region_0.1 | all-reduce | flops 32768 | bytes 196608 | tf_op jit(solution)/shard_map/psum | solution.py:113
  66.6 8.0 %collective-permute-start.3 = (bf16[512,1,128]{2,0,1:T(8,128)(2,1)}, bf16[512,1,128]{2,0,1:T(8,128)(2,1)}, u32[]{:S(2)}, u32[]{:S(2)}) collective-permute-start(bf16[512,1,128]{2,0,1:T(8,128)(2,1)} %get-tuple-element.120), channel_id=1, source_target_pairs={{16,0},{32,16},{48,32},{64,48},{80,64},{96,80},{112,96},{128,112},... | collective-permute-start | bytes 393224 | tf_op jit(solution)/shard_map/ppermute | solution.py:17
  81.6 3.2 collective-permute-start
  85.7 2.4 fusion.52
  95.0 1.8 copy.41
  107.7 4.5 %fusion.46 = (bf16[4,1024,128]{1,2,0:T(8,128)(2,1)}, bf16[4,1024,128]{1,2,0:T(8,128)(2,1)}, bf16[4,1024,128]{1,2,0:T(8,128)(2,1)}, bf16[4,1024,128]{1,2,0:T(8,128)(2,1)}) fusion(bf16[512,4,128]{0,2,1:T(8,128)(2,1)S(1)} %reshape.270, bf16[512,4,128]{0,2,1:T(8,128)(2,1)S(1)} %reshape.269, pred[4]{0:T(512)(128)(4,1)S(1)} %copy-done.23, ...), kind=kLoop, calls=%fused_computation.65 | loop fusion | flops 12582912 | bytes 11010052 | tf_op jit(solution)/shard_map/transpose | solution.py:180
  112.2 57.7 %while.14 = (s32[]{:T(128)}, f32[4,1024,128]{1,2,0:T(8,128)}, f32[4,1024,128]{1,2,0:T(8,128)}, bf16[4,1024,128]{1,2,0:T(8,128)(2,1)}, bf16[4,1024,128]{1,2,0:T(8...) while((s32[]{:T(128)}, f32[4,1024,128]{1,2,0:T(8,128)}, ...), condition=%wide.region_6.7_spmd, body=%wide.region_2.6_spmd.sunk | while | flops 1373107200 | bytes 47235736 | solution.py:183
  112.2 1.8 fusion.112
  117.7 4.0 fusion.115
  122.7 3.9 fusion.116
  132.1 4.0 fusion.115
  137.2 3.9 fusion.116
  146.5 4.0 fusion.115
  151.6 3.9 fusion.116
  160.9 4.0 fusion.115
  166.0 4.0 fusion.116
  169.9 3.8 select_reduce_fusion.1
  173.8 2.7 collective-permute-start.5
  177.3 6.5 %collective-permute-done.5 = f32[1,512,128]{1,2,0:T(8,128)S(1)} collective-permute-done((f32[1,512,128]{1,2,0:T(8,128)S(1)}, f32[1,512,128]{1,2,0:T(8,128)S(1)}, u32[]{:S(2)}, u32[]{:S(2)}) %collective-permute-start.5) | collective-permute-done | bytes 262176 | tf_op jit(solution)/shard_map/ppermute | solution.py:17
  187.8 21.0 %collective-permute-done.4 = f32[4,512,128]{1,2,0:T(8,128)S(1)} collective-permute-done((f32[4,512,128]{1,2,0:T(8,128)}, f32[4,512,128]{1,2,0:T(8,128)S(1)}, u32[]{:S(2)}, u32[]{:S(2)}) %collective-permute-start.4) | collective-permute-done | bytes 1048608 | tf_op jit(solution)/shard_map/ppermute | solution.py:17
  210.4 60.8 %all-reduce.11 = (bf16[1024,16]{0,1:T(8,128)(2,1)S(1)}, bf16[1024,16]{0,1:T(8,128)(2,1)S(1)}) all-reduce(f32[1024,16]{0,1:T(8,128)S(1)} %convolution_multiply_fusion.2, f32[1024,16]{0,1:T(8,128)S(1)} %convolution_multiply_fusion.3), channel_id=1, replica_groups=mesh['ctx'=16,'head'=16] {'head'}, use_global_device_ids=true, to_apply=%region_7.8 | all-reduce | flops 32768 | bytes 196608 | tf_op jit(solution)/shard_map/psum | solution.py:221
  274.6 35.9 %all-gather.2.cloned.1.call-done = f32[256,16,1024]{2,1,0:T(8,128)} async-done(((f32[1,16,1024]{2,1,0:T(8,128)}), f32[256,16,1024]{2,1,0:T(8,128)}) %all-gather.2.cloned.1.call-update) | async-done | bytes 16777232 | tf_op jit(solution)/shard_map/all_gather | solution.py:233
  310.6 7.3 %reduce_sum.50 = f32[16,1024]{1,0:T(8,128)} reduce(f32[256,16,1024]{2,1,0:T(8,128)} %all-gather.2.cloned.1.call-done, f32[]{:T(128)} %constant.108.clone.1), dimensions={0}, to_apply=%region_14.15 | reduce | flops 4177920 | bytes 16842756 | tf_op jit(solution)/shard_map/reduce_sum | solution.py:233
  317.9 117.4 %all-reduce.9.cloned.1.call-done = (f32[512,16]{0,1:T(8,128)}, f32[16,512]{1,0:T(8,128)}, f32[512,16]{0,1:T(8,128)}) async-done(((f32[512,16]{0,1:T(8,128)}, f32[16,512]{1,0:T(8,128)}, f32[512,16]{0,1:T(8,128)}), (f32[512,16]{0,1:T(8,128)}, f32[16,512]{1,0:T(8,128)}, f32[512,16]{0,1:T(8,128)})) %all-reduce.9.cloned.1.call-update) | async-done | bytes 98320 | tf_op jit(solution)/shard_map/psum | solution.py:230
  (136 shorter events, 69.1 us)
Async XLA Ops:
  8.0 66.6 %copy-start.15 = (bf16[1024,512]{1,0:T(8,128)(2,1)S(1)}, bf16[1024,512]{1,0:T(8,128)(2,1)}, u32[]{:S(2)}) copy-start(bf16[1024,512]{1,0:T(8,128)(2,1)} %param.24) | copy-start | bytes 3145732
  8.0 302.5 %all-gather.2.cloned.1.call-start = ((), (), s32[]{:S(2)}) async-start(), calls=%async_computation | async-start | bytes 16842752 | tf_op jit(solution)/shard_map/all_gather | solution.py:233
  64.5 2.1 copy-start.20
  64.5 15.1 %copy-start.18 = (bf16[1024,16]{0,1:T(8,128)(2,1)}, bf16[1024,16]{0,1:T(8,128)(2,1)S(1)}, u32[]{:S(2)}) copy-start(bf16[1024,16]{0,1:T(8,128)(2,1)S(1)} %get-tuple-element.98) | copy-start | bytes 98308
  66.6 34.8 %collective-permute-start.3 = (bf16[512,1,128]{2,0,1:T(8,128)(2,1)}, bf16[512,1,128]{2,0,1:T(8,128)(2,1)}, u32[]{:S(2)}, u32[]{:S(2)}) collective-permute-start(bf16[512,1,128]{2,0,1:T(8,128)(2,1)} %get-tuple-element.120), channel_id=1, source_target_pairs={{16,0},{32,16},{48,32},{64,48},{80,64},{96,80},{112,96},{128,112},... | collective-permute-start | bytes 393224 | tf_op jit(solution)/shard_map/ppermute | solution.py:17
  75.2 4.4 copy-start.22
  76.3 28.4 %collective-permute-start.2 = (bf16[512,4,128]{0,2,1:T(8,128)(2,1)}, bf16[512,4,128]{0,2,1:T(8,128)(2,1)}, u32[]{:S(2)}, u32[]{:S(2)}) collective-permute-start(bf16[512,4,128]{0,2,1:T(8,128)(2,1)} %bitcast.15), channel_id=1, source_target_pairs={{16,0},{32,16},{48,32},{64,48},{80,64},{96,80},{112,96},{128,112},... | collective-permute-start | bytes 1572872 | tf_op jit(solution)/shard_map/ppermute | solution.py:17
  81.6 23.1 %collective-permute-start = (bf16[512,4,128]{0,2,1:T(8,128)(2,1)}, bf16[512,4,128]{0,2,1:T(8,128)(2,1)}, u32[]{:S(2)}, u32[]{:S(2)}) collective-permute-start(bf16[512,4,128]{0,2,1:T(8,128)(2,1)} %get-tuple-element.116), channel_id=1, source_target_pairs={{16,0},{32,16},{48,32},{64,48},{80,64},{96,80},{112,96},{128,112},... | collective-permute-start | bytes 1572872 | tf_op jit(solution)/shard_map/ppermute | solution.py:17
  89.6 13.4 %collective-permute-start.1 = (bf16[512,1,128]{2,0,1:T(8,128)(2,1)}, bf16[512,1,128]{2,0,1:T(8,128)(2,1)}, u32[]{:S(2)}, u32[]{:S(2)}) collective-permute-start(bf16[512,1,128]{2,0,1:T(8,128)(2,1)} %pad_maximum_fusion.3), channel_id=1, source_target_pairs={{16,0},{32,16},{48,32},{64,48},{80,64},{96,80},{112,96},{128,112},... | collective-permute-start | bytes 393224 | tf_op jit(solution)/shard_map/ppermute | solution.py:17
  98.5 9.2 %copy-start.13 = (bf16[1024,128]{0,1:T(8,128)(2,1)S(1)}, bf16[1024,128]{0,1:T(8,128)(2,1)}, u32[]{:S(2)}) copy-start(bf16[1024,128]{0,1:T(8,128)(2,1)} %copy.47) | copy-start | bytes 786436
  104.7 3.0 copy-start.11
  104.7 3.0 copy-start.12
  104.7 3.0 copy-start.14
  104.7 3.0 copy-start.23
  112.2 57.7 %copy-start.24 = (pred[4]{0:T(512)(128)(4,1)S(1)}, pred[4]{0:T(512)(128)(4,1)}, u32[]{:S(2)}) copy-start(pred[4]{0:T(512)(128)(4,1)} %broadcast_compare_fusion) | copy-start | bytes 16
  169.9 6.6 %copy-start.2 = (f32[4,1024,128]{1,2,0:T(8,128)S(1)}, f32[4,1024,128]{1,2,0:T(8,128)}, u32[]{:S(2)}) copy-start(f32[4,1024,128]{1,2,0:T(8,128)} %get-tuple-element.66) | copy-start | bytes 6291460
  169.9 6.6 %copy-start.3 = (f32[4,1024,128]{1,2,0:T(8,128)S(1)}, f32[4,1024,128]{1,2,0:T(8,128)}, u32[]{:S(2)}) copy-start(f32[4,1024,128]{1,2,0:T(8,128)} %get-tuple-element.67) | copy-start | bytes 6291460
  173.8 10.0 %collective-permute-start.5 = (f32[1,512,128]{1,2,0:T(8,128)S(1)}, f32[1,512,128]{1,2,0:T(8,128)S(1)}, u32[]{:S(2)}, u32[]{:S(2)}) collective-permute-start(f32[1,512,128]{1,2,0:T(8,128)S(1)} %bitcast.129), channel_id=1, source_target_pairs={{240,0},{0,16},{16,32},{32,48},{48,64},{64,80},{80,96},{96,112},{1... | collective-permute-start | bytes 786440 | tf_op jit(solution)/shard_map/ppermute | solution.py:17
  176.5 8.1 %copy-start.21 = (bf16[1024,16]{0,1:T(8,128)(2,1)S(1)}, bf16[1024,16]{0,1:T(8,128)(2,1)}, u32[]{:S(2)}) copy-start(bf16[1024,16]{0,1:T(8,128)(2,1)} %copy-done.20) | copy-start | bytes 98308
  184.7 24.4 %copy-start.7 = (f32[1024,64]{0,1:T(8,128)S(1)}, f32[1024,64]{0,1:T(8,128)}, u32[]{:S(2)}) copy-start(f32[1024,64]{0,1:T(8,128)} %copy-done.6) | copy-start | bytes 786436
  185.7 249.6 %all-reduce.9.cloned.1.call-start = ((), (), s32[]{:S(2)}) async-start(), calls=%async_computation.1 | async-start | bytes 196608 | tf_op jit(solution)/shard_map/psum | solution.py:230
  185.7 23.4 %copy-start.9 = (f32[1024,64]{0,1:T(8,128)S(1)}, f32[1024,64]{0,1:T(8,128)}, u32[]{:S(2)}) copy-start(f32[1024,64]{0,1:T(8,128)} %copy-done.8) | copy-start | bytes 786436
  185.7 23.1 %collective-permute-start.4 = (f32[4,512,128]{1,2,0:T(8,128)}, f32[4,512,128]{1,2,0:T(8,128)S(1)}, u32[]{:S(2)}, u32[]{:S(2)}) collective-permute-start(f32[4,512,128]{1,2,0:T(8,128)} %get-tuple-element.124), channel_id=1, source_target_pairs={{240,0},{0,16},{16,32},{32,48},{48,64},{64,80},{80,96},{96,112},{1... | collective-permute-start | bytes 3145736 | tf_op jit(solution)/shard_map/ppermute | solution.py:17
  209.6 63.3 %copy-start.19 = (bf16[1024,16]{0,1:T(8,128)(2,1)S(1)}, bf16[1024,16]{0,1:T(8,128)(2,1)}, u32[]{:S(2)}) copy-start(bf16[1024,16]{0,1:T(8,128)(2,1)} %copy-done.18) | copy-start | bytes 98308
  (15 other events, 21.7 us)
Sparse Core Ops, SparseCore 0:
  185.8 124.7 all-gather.1
Sparse Core Ops, SparseCore 1:
  274.7 160.5 all-reduce.8
